TPU v7x, 32 devices: a whole 2x2x4 slice. The times are simulated.
32 devices in a mesh: groups: 2 (over x), dp: 8 (over z, y), split: 2 (over core).
Axes of the slice: x: 2, y: 2, z: 4, core: 2. Of those that a mesh axis runs over, the one named last changes fastest.
Arguments:
- embeddings: bfloat16 [65536, 512], P(('groups', 'dp', 'split')), parts along dimension 0, may hold values from -6 to 6
- assignment: int32 [65536, 1], P(('groups', 'dp', 'split')), parts along dimension 0, may hold values from 0 to 15; in each aligned block of 2048 rows (0 to 2047, 2048 to 4095, ...) at most 192 rows name the same one
- order_key: int32 [65536], P(('groups', 'dp', 'split')), parts along dimension 0, may hold values from 0 to 32767, each once
Outputs:
- nearest: float32 [65536], P(('groups', 'dp', 'split')), parts along dimension 0
There are 2 independent parts, one for each index of `groups`. A program takes and returns all parts, laid end to end along the dimension named above; each array names one. Nothing has to cross between parts.
Inputs may be any that keep to these rules, and one draw needn't show every extreme that they name: `assignment`: in each device's 2048 rows no cluster has more than 192 rows, and some cluster has exactly 192. `order_key`: all values within a part are distinct.
All inputs are finite; a program needn't handle non-finite values.
Results may differ from a plain program's by a relative error of at most 0.0013.
Values may be sent and summed in bfloat16 or wider, within the bound.
A program may use at most 64 MiB of HBM per device.

v0:
```python
import jax
import jax.numpy as jnp
from jax import lax
from jax.sharding import PartitionSpec as P

CL_OWN = 2


empty_key = 1 << 30
epsilon = 1e-06


def as_sent(value):
    return jax.tree.map(lambda a: a.astype(jnp.bfloat16) if a.dtype == jnp.float32 else a, value)


def unit_rows(embeddings):
    values = embeddings.astype(jnp.float32)
    scale = lax.rsqrt(jnp.sum(values * values, axis=1, keepdims=True) + epsilon)
    return (values * scale).astype(jnp.bfloat16)


def by_cluster(rows, keys):
    sources, count, most, width = rows.shape
    own = jnp.moveaxis(rows, 1, 0).reshape(count, sources * most, width)
    own_key = jnp.moveaxis(keys, 1, 0).reshape(count, sources * most)
    return (own, own_key)


def tile_max(best, own, own_key, cols, col_key):
    count, length, width = own.shape
    half = length // 2
    own_blocks = own.reshape(count * 2, half, width)
    key_blocks = own_key.reshape(count * 2, half)
    best_blocks = best.reshape(count * 2, half)

    def step(index):
        which = index // 2
        sims = lax.dot_general(
            own_blocks[index],
            cols[which],
            (((1,), (1,)), ((), ())),
            preferred_element_type=jnp.float32,
        )
        allowed = col_key[which][None, :] < key_blocks[index][:, None]
        return jnp.maximum(best_blocks[index], jnp.max(jnp.where(allowed, sims, -1.0), axis=1))

    return lax.map(step, jnp.arange(count * 2)).reshape(count, length)


def per_device(embeddings, assignment, order_key):
    rows_dev, width = embeddings.shape
    n_dp = lax.axis_size("dp")
    clusters = CL_OWN * n_dp
    most = 3 * rows_dev // (2 * clusters)
    cluster = assignment[:, 0]
    onehot = cluster[:, None] == jnp.arange(clusters, dtype=jnp.int32)[None, :]
    running = jnp.cumsum(onehot.astype(jnp.int32), axis=0)
    rank = jnp.sum(jnp.where(onehot, running, 0), axis=1) - 1
    slot = cluster * most + rank
    unit = unit_rows(embeddings)
    flat_rows = jnp.zeros((clusters * most, width), jnp.bfloat16).at[slot].set(unit)
    flat_keys = jnp.full((clusters * most,), empty_key, jnp.int32).at[slot].set(order_key)
    send_rows = flat_rows.reshape(n_dp, CL_OWN, most, width)
    send_keys = flat_keys.reshape(n_dp, CL_OWN, most)
    got_rows = lax.all_to_all(send_rows, "dp", split_axis=0, concat_axis=0, tiled=True)
    got_keys = lax.all_to_all(send_keys, "dp", split_axis=0, concat_axis=0, tiled=True)
    count = got_rows.shape[1]
    own, own_key = by_cluster(got_rows, got_keys)
    start_best = jnp.full(own_key.shape, -1.0, jnp.float32)
    best = tile_max(
        start_best,
        own,
        own_key,
        lax.all_gather(own, "split", axis=1, tiled=True),
        lax.all_gather(as_sent(own_key), "split", axis=1, tiled=True),
    )
    maxima = jnp.moveaxis(best.reshape(count, n_dp, most), 0, 1)
    returned = lax.all_to_all(maxima, "dp", split_axis=0, concat_axis=0, tiled=True)
    return returned.reshape(clusters * most)[slot]


def solution(mesh):
    placed = (
        P(("groups", "dp", "split"), None),
        P(("groups", "dp", "split"), None),
        P(("groups", "dp", "split")),
    )
    return jax.shard_map(
        per_device,
        mesh=mesh,
        in_specs=placed,
        out_specs=P(("groups", "dp", "split")),
        check_vma=False,
    )
```

profile of v0, /device:TPU:0, one launch (start us, length us, event | category | flops | bytes accessed | tf_op | source)
XLA Modules:
  0.0 204.7 jit_solution(2776743660190105068)
XLA Ops:
  6.5 0.0 all-gather.2.cloned.1.call-start
  6.5 0.7 fusion.13
  7.2 4.5 %reduce-window.6 = s32[16,16,128]{2,1,0:T(8,128)S(1)} reduce-window(s32[16,16,128]{2,1,0:T(8,128)S(1)} %fusion.13, s32[]{:T(128)} %constant.69.clone.1), window={size=1x1x128 pad=0_0x0_0x127_0}, to_apply=%region_0.0 | reduce-window | flops 4161536 | bytes 262148 | tf_op jit(solution)/shard_map/reduce-window
  11.8 0.4 slice_reduce_fusion
  12.2 0.2 reduce-window.9
  12.4 0.1 broadcast_add_fusion
  12.5 0.8 fusion.12
  13.3 0.7 compare_select_fusion
  14.0 2.1 %fusion.5 = f32[2048]{0:T(1024)S(1)} fusion(bf16[2048,512]{1,0:T(8,128)(2,1)} %param.5), kind=kLoop, calls=%fused_computation.14 | loop fusion | flops 3143680 | bytes 2105344 | tf_op jit(solution)/shard_map/reduce_sum | solution.py:19
  16.1 11.8 %scatter_custom_fusion.1 = bf16[3072,512]{1,0:T(8,128)(2,1)S(1)} fusion(s32[2048]{0:T(1024)S(1)} %bitcast.51, bf16[2048,512]{1,0:T(8,128)(2,1)} %param.5, f32[2048]{0:T(1024)S(1)} %add_rsqrt_fusion, bf16[]{:T(256)} %constant.71.clone.1), kind=kCustom, calls=%fused_computation.16 | custom fusion | flops 3145728 | bytes 5251074 | tf_op jit(solution)/shard_map/scatter | solution.py:62
  27.9 77.8 %all_to_all.15 = bf16[8,2,192,512]{3,2,1,0:T(8,128)(2,1)S(1)} all-to-all(bf16[8,2,192,512]{3,2,1,0:T(8,128)(2,1)S(1)} %bitcast.45), channel_id=1, replica_groups=mesh['groups'=2,'dp'=8,'split'=2] {'dp'}, dimensions={0} | all-to-all | bytes 6291456 | tf_op jit(solution)/shard_map/all_to_all | solution.py:66
  105.7 2.0 copy.7
  107.7 0.0 all-gather.2.cloned.1.call-update
  107.7 8.2 %scatter_custom_fusion = s32[3072]{0:T(1024)S(1)} fusion(s32[2048]{0:T(1024)S(1)} %bitcast.52, s32[2048]{0:T(1024)} %param.7, s32[]{:T(128)} %constant.76.clone.1), kind=kCustom, calls=%fused_computation.30 | custom fusion | bytes 12800 | tf_op jit(solution)/shard_map/scatter | solution.py:63
  116.0 0.7 reshape.60
  116.6 3.6 %all-to-all-start = ((s32[8,2,192]{2,1,0:T(2,128)}), s32[8,2,192]{2,1,0:T(2,128)S(1)}, u32[]{:S(2)}, u32[]{:S(2)}) async-start(s32[8,2,192]{2,1,0:T(2,128)} %reshape.60), calls=%async_computation | async-start | bytes 32768 | tf_op jit(solution)/shard_map/all_to_all | solution.py:67
  120.2 6.6 %all-to-all-done = s32[8,2,192]{2,1,0:T(2,128)S(1)} async-done(((s32[8,2,192]{2,1,0:T(2,128)}), s32[8,2,192]{2,1,0:T(2,128)S(1)}, u32[]{:S(2)}, u32[]{:S(2)}) %all-to-all-start) | async-done | bytes 12320 | tf_op jit(solution)/shard_map/all_to_all | solution.py:67
  126.8 0.1 reshape.61
  126.9 0.1 reshape_reshape.9
  127.0 1.8 all_gather.6
  128.8 0.0 all-gather.2.cloned.1.call-done
  128.8 37.9 %while.12 = (s32[]{:T(128)}, f32[4,768]{1,0:T(4,128)S(1)}, s32[4]{0:T(128)S(1)}, s32[2,3072]{1,0:T(2,128)S(1)}, s32[4,768]{1,0:T(4,128)S(1)}, /*index=5*/bf16[4,...) while((s32[]{:T(128)}, f32[4,768]{1,0:T(4,128)S(1)}, ...), condition=%wide.region_8.9_spmd, body=%wide.region_6.8_spmd.sunk | while | flops 2422996992 | bytes 4000102 | solution.py:48
  128.8 0.6 dynamic_slice.50
  133.3 4.9 %select_reduce_fusion.2 = f32[768]{0:T(1024)S(1)} fusion(s32[3072]{0:T(1024)S(1)} %bitcast.47, s32[768]{0:T(1024)S(1)} %dynamic-slice_reduce_fusion.2, bf16[2,3072,512]{2,1,0:T(8,128)(2,1)} %get-tuple-element.183, s32[]{:T(128)S(6)} %select_n.52, bf16[4,768,512]{2,1,0:T(8,128)(2,1)} %get-tuple-element.182, s32[]{:T(128)S(6)} %select_n.53), kind=kOutput, calls=%fused_computation.3.clone.1 | convolution fusion | flops 2422996224 | bytes 3950600 | tf_op jit(solution)/shard_map/while/body/eval_jaxpr/dot_general | solution.py:39
  138.2 0.1 dynamic_update_slice.8
  138.3 0.6 dynamic_slice.50
  142.8 4.9 %select_reduce_fusion.2 = f32[768]{0:T(1024)S(1)} fusion(s32[3072]{0:T(1024)S(1)} %bitcast.47, s32[768]{0:T(1024)S(1)} %dynamic-slice_reduce_fusion.2, bf16[2,3072,512]{2,1,0:T(8,128)(2,1)} %get-tuple-element.183, s32[]{:T(128)S(6)} %select_n.52, bf16[4,768,512]{2,1,0:T(8,128)(2,1)} %get-tuple-element.182, s32[]{:T(128)S(6)} %select_n.53), kind=kOutput, calls=%fused_computation.3.clone.1 | convolution fusion | flops 2422996224 | bytes 3950600 | tf_op jit(solution)/shard_map/while/body/eval_jaxpr/dot_general | solution.py:39
  147.7 0.1 dynamic_update_slice.8
  147.8 0.6 dynamic_slice.50
  152.2 4.9 %select_reduce_fusion.2 = f32[768]{0:T(1024)S(1)} fusion(s32[3072]{0:T(1024)S(1)} %bitcast.47, s32[768]{0:T(1024)S(1)} %dynamic-slice_reduce_fusion.2, bf16[2,3072,512]{2,1,0:T(8,128)(2,1)} %get-tuple-element.183, s32[]{:T(128)S(6)} %select_n.52, bf16[4,768,512]{2,1,0:T(8,128)(2,1)} %get-tuple-element.182, s32[]{:T(128)S(6)} %select_n.53), kind=kOutput, calls=%fused_computation.3.clone.1 | convolution fusion | flops 2422996224 | bytes 3950600 | tf_op jit(solution)/shard_map/while/body/eval_jaxpr/dot_general | solution.py:39
  157.1 0.1 dynamic_update_slice.8
  157.2 0.6 dynamic_slice.50
  161.7 4.9 %select_reduce_fusion.2 = f32[768]{0:T(1024)S(1)} fusion(s32[3072]{0:T(1024)S(1)} %bitcast.47, s32[768]{0:T(1024)S(1)} %dynamic-slice_reduce_fusion.2, bf16[2,3072,512]{2,1,0:T(8,128)(2,1)} %get-tuple-element.183, s32[]{:T(128)S(6)} %select_n.52, bf16[4,768,512]{2,1,0:T(8,128)(2,1)} %get-tuple-element.182, s32[]{:T(128)S(6)} %select_n.53), kind=kOutput, calls=%fused_computation.3.clone.1 | convolution fusion | flops 2422996224 | bytes 3950600 | tf_op jit(solution)/shard_map/while/body/eval_jaxpr/dot_general | solution.py:39
  166.6 0.1 dynamic_update_slice.8
  166.7 0.1 reshape_reshape.11
  166.8 0.6 copy.13
  167.4 3.3 %all-to-all-start.2 = ((f32[8,2,192]{2,1,0:T(2,128)}), f32[8,2,192]{2,1,0:T(2,128)S(1)}, u32[]{:S(2)}, u32[]{:S(2)}) async-start(f32[8,2,192]{2,1,0:T(2,128)} %bitcast.32), calls=%async_computation.2 | async-start | bytes 32768 | tf_op jit(solution)/shard_map/all_to_all | solution.py:79
  170.7 6.5 %all-to-all-done.2 = f32[8,2,192]{2,1,0:T(2,128)S(1)} async-done(((f32[8,2,192]{2,1,0:T(2,128)}), f32[8,2,192]{2,1,0:T(2,128)S(1)}, u32[]{:S(2)}, u32[]{:S(2)}) %all-to-all-start.2) | async-done | bytes 12320 | tf_op jit(solution)/shard_map/all_to_all | solution.py:79
  177.2 0.1 reshape.64
  177.3 20.5 %gather_fusion = f32[2048]{0:T(1024)} fusion(f32[3072]{0:T(1024)S(1)} %reshape.64, s32[2048]{0:T(1024)S(1)} %broadcast_clamp_fusion), kind=kCustom, calls=%fused_computation | custom fusion | bytes 24576 | tf_op jit(solution)/shard_map/gather | solution.py:80
  (22 shorter events, 0.2 us)
Async XLA Ops:
  6.5 122.3 %all-gather.2.cloned.1.call-start = ((), (), s32[]{:S(2)}) async-start(), calls=%async_computation.3 | async-start | bytes 9437184 | tf_op jit(solution)/shard_map/all_gather | solution.py:75
  116.6 10.2 %all-to-all-start = ((s32[8,2,192]{2,1,0:T(2,128)}), s32[8,2,192]{2,1,0:T(2,128)S(1)}, u32[]{:S(2)}, u32[]{:S(2)}) async-start(s32[8,2,192]{2,1,0:T(2,128)} %reshape.60), calls=%async_computation | async-start | bytes 32768 | tf_op jit(solution)/shard_map/all_to_all | solution.py:67
  167.4 9.9 %all-to-all-start.2 = ((f32[8,2,192]{2,1,0:T(2,128)}), f32[8,2,192]{2,1,0:T(2,128)S(1)}, u32[]{:S(2)}, u32[]{:S(2)}) async-start(f32[8,2,192]{2,1,0:T(2,128)} %bitcast.32), calls=%async_computation.2 | async-start | bytes 32768 | tf_op jit(solution)/shard_map/all_to_all | solution.py:79
Sparse Core Ops, SparseCore 0:
  107.8 15.7 all-gather.1
where the time goes:
time: 205 us
  blocking collectives  79.6 us (39%)
  local copies, waits for them, and re-layouts  35.7 us (17%)
  other arithmetic  20.9 us (10%)
  matrix products  19.5 us (10%)
  loops' own time  15.3 us (7%)
  between operations  13.5 us (7%)
  waiting for transfers between devices  13.1 us (6%)
  starting transfers between devices  6.93 us (3%)
    all_to_all x1, blocking collectives, per_device(): lax.all_to_all(send_rows, 'dp', split_axis=0, concat_axis=0, tiled=True)  77.8 us
    gather x1, local copies, waits for them, and re-layouts, per_device(): return returned.reshape(clusters * most)[slot]  20.5 us
    dot_general x4, matrix products, step(): lax.dot_general(own_blocks[index], cols[which], (((1,), (1,)), ((), ())),...  19.5 us
    another operation x1, loops' own time, tile_max(): return lax.map(step, jnp.arange(count * 2)).reshape(count, length)  15.3 us
    scatter x1, other arithmetic, per_device(): jnp.zeros((clusters * most, width), jnp.bfloat16).at[slot].set(unit)  11.8 us
    scatter x1, local copies, waits for them, and re-layouts, per_device(): jnp.full((clusters * most,), empty_key, jnp.int32).at[slot].set(order_key)  8.22 us
    all_to_all x1, waiting for transfers between devices, per_device(): lax.all_to_all(send_keys, 'dp', split_axis=0, concat_axis=0, tiled=True)  6.57 us
    all_to_all x1, waiting for transfers between devices, per_device(): lax.all_to_all(maxima, 'dp', split_axis=0, concat_axis=0, tiled=True)  6.5 us
  transfers between devices with their start and end apart: 3, of which 2 were waited for; matrix products, arithmetic and copies ran while one was open for 4% of the time, Pallas kernels for 0%

commit v1 on v0

v1 whole, which is shorter than its diff:
```python
import functools

import jax
import jax.numpy as jnp
from jax import lax
from jax.experimental import pallas as pl
from jax.experimental.pallas import tpu as pltpu
from jax.sharding import PartitionSpec as P

epsilon = 1e-06
MESH = pl.DeviceIdType.MESH
NT = (((1,), (1,)), ((), ()))
BLOCK = 256
SUB = 8


def xor(a, b, n):
    total, bit = 0, 1
    while bit < n:
        p, q = (a // bit) % 2, (b // bit) % 2
        total = total + (p + q - 2 * p * q) * bit
        bit *= 2
    return total


def offset_of(slot, n):
    t = slot - 1
    near = t % 2
    return (1 - near) * (n // 2 + t // 2) + near * ((t + 1) // 2 % (n // 2))


def kernel(n, n_split, most, rows_ref, cluster_ref, key_ref, out_ref,
           slot_ref, send, send_key, recv, recv_key, lane_key, sub_key, best, back_send, back,
           row_ssem, row_rsem, key_ssem, key_rsem, back_ssem, back_rsem):
    f32, bf16, i32 = jnp.float32, jnp.bfloat16, jnp.int32
    rows = rows_ref.shape[0]
    me = lax.axis_index("dp") * n_split + lax.axis_index("split")

    def device(slot):
        partner = xor(me, offset_of(slot, n), n)
        return {"dp": partner // n_split, "split": partner % n_split}

    barrier = pltpu.get_barrier_semaphore()

    @pl.loop(1, n)
    def _(slot):
        pl.semaphore_signal(barrier, inc=1, device_id=device(slot), device_id_type=MESH)

    before = (lax.broadcasted_iota(i32, (BLOCK, BLOCK), 0) < lax.broadcasted_iota(i32, (BLOCK, BLOCK), 1))
    before = jnp.where(before, 1.0, 0.0).astype(bf16)
    carry = jnp.zeros((n, 1), f32)
    for start in range(0, rows, BLOCK):
        here = cluster_ref[:, start:start + BLOCK]
        onehot = jnp.where(lax.broadcasted_iota(i32, (n, BLOCK), 0) == here, 1.0, 0.0)
        earlier = jnp.dot(onehot.astype(bf16), before, preferred_element_type=f32) + carry
        carry = carry + jnp.sum(onehot, axis=1, keepdims=True)
        rank = jnp.sum(onehot * earlier, axis=0, keepdims=True).astype(i32)
        slot_ref[:, start:start + BLOCK] = here * most + rank

    key = key_ref[...]
    digit = lax.broadcasted_iota(i32, (SUB, rows), 0)
    digits = jnp.where(digit == 0, key // 16384, jnp.where(digit == 1, (key // 128) % 128, jnp.where(digit == 2, key % 128, jnp.where(digit == 3, 1, 0))))
    digits = digits.astype(f32).astype(bf16)

    def weights(shape, dim):
        place = lax.broadcasted_iota(i32, shape, dim)
        w = jnp.where(place == 0, 16384.0, jnp.where(place == 1, 128.0, jnp.where(place == 2, 1.0, jnp.where(place == 3, -4194304.0, 0.0))))
        return w.astype(bf16)

    same = lax.broadcasted_iota(i32, (most, most), 0) == lax.broadcasted_iota(i32, (most, most), 1)
    identity = jnp.where(same, 1.0, 0.0).astype(bf16)

    def pack(cluster):
        place = slot_ref[...] - cluster * most
        pick = jnp.where(lax.broadcasted_iota(i32, (most, rows), 0) == place, 1.0, 0.0).astype(bf16)
        values = jnp.dot(pick, rows_ref[...], preferred_element_type=f32)
        scale = lax.rsqrt(jnp.sum(values * values, axis=1, keepdims=True) + epsilon)
        return (values * scale).astype(bf16), lax.dot_general(digits, pick, NT, preferred_element_type=f32)

    def row_copy(slot):
        return pltpu.make_async_remote_copy(send.at[slot], recv.at[slot], row_ssem.at[slot], row_rsem.at[slot], device_id=device(slot), device_id_type=MESH)

    def key_copy(slot):
        return pltpu.make_async_remote_copy(send_key.at[slot], recv_key.at[slot], key_ssem.at[slot], key_rsem.at[slot], device_id=device(slot), device_id_type=MESH)

    def back_copy(slot, cluster):
        return pltpu.make_async_remote_copy(back_send.at[slot], back.at[cluster], back_ssem.at[slot], back_rsem.at[slot], device_id=device(slot), device_id_type=MESH)

    send[1], send_key[1] = pack(xor(me, offset_of(1, n), n))
    pl.semaphore_wait(barrier, n - 1)

    @pl.loop(2, n + 1)
    def _(slot):
        row_copy(slot - 1).start()
        key_copy(slot - 1).start()
        at = slot % n
        packed, packed_key = pack(xor(me, offset_of(slot, n), n))
        send[at] = packed
        send_key[at] = packed_key

    def take(slot, new, digits_in):
        parts = digits_in.astype(bf16)
        lane_key[slot] = jnp.dot(weights((SUB, SUB), 1), parts, preferred_element_type=f32)
        turned = lax.dot_general(identity, parts, NT, preferred_element_type=f32).astype(bf16)
        sub_key[slot] = jnp.dot(turned, weights((SUB, 128), 0), preferred_element_type=f32)

    def tile(columns, columns_key, own, own_key):
        sims = lax.dot_general(columns, own, NT, preferred_element_type=f32)
        seen = jnp.where(columns_key < own_key, sims, -1.0)
        return jnp.max(seen.reshape(most // SUB, SUB, most), axis=0)

    recv[0] = send[0]
    take(0, send[0], send_key[0])
    best[0] = jnp.maximum(tile(recv[0], sub_key[0][:, :1], recv[0], lane_key[0][:1]), -1.0)

    @pl.loop(1, n)
    def _(u):
        row_copy(u).wait_recv()
        key_copy(u).wait_recv()
        new = recv[u]
        take(u, new, recv_key[u])
        new_lane, new_sub = lane_key[u][:1], sub_key[u][:, :1]

        def meet(i, running):
            other = recv[i]
            best[i] = jnp.maximum(best[i], tile(new, new_sub, other, lane_key[i][:1]))
            return jnp.maximum(running, tile(other, sub_key[i][:, :1], new, new_lane))

        best[u] = lax.fori_loop(0, u, meet, tile(new, new_sub, new, new_lane))

    part = lax.broadcasted_iota(i32, (SUB, most), 0)

    def parts_of(slot):
        whole = jnp.broadcast_to(jnp.max(best[slot], axis=0, keepdims=True), (SUB, most))
        high = whole.astype(bf16).astype(f32)
        middle = (whole - high).astype(bf16).astype(f32)
        low = (whole - high) - middle
        return jnp.where(part == 0, high, jnp.where(part == 1, middle, jnp.where(part == 2, low, 0.0)))

    @pl.loop(1, n)
    def _(slot):
        back_send[slot] = parts_of(slot)

    back[me] = parts_of(0)

    @pl.loop(1, n)
    def _(slot):
        back_copy(slot, me).start()

    @pl.loop(1, n)
    def _(slot):
        row_copy(slot).wait_send()
        key_copy(slot).wait_send()

    @pl.loop(1, n)
    def _(slot):
        back_copy(slot, xor(me, offset_of(slot, n), n)).wait_recv()

    turned = lax.dot_general(identity, back[...].reshape(n * SUB, most).astype(bf16), NT, preferred_element_type=f32).astype(bf16)
    for start in range(0, rows, BLOCK):
        here = cluster_ref[:, start:start + BLOCK]
        rank = slot_ref[:, start:start + BLOCK] - here * most
        onehot = jnp.where(lax.broadcasted_iota(i32, (n * SUB, BLOCK), 0) // SUB == here, 1.0, 0.0).astype(bf16)
        found = jnp.dot(turned, onehot, preferred_element_type=f32)
        found = jnp.where(lax.broadcasted_iota(i32, (most, BLOCK), 0) == rank, found, 0.0)
        out_ref[:, start:start + BLOCK] = jnp.sum(found, axis=0, keepdims=True)

    @pl.loop(1, n)
    def _(slot):
        back_copy(slot, me).wait_send()


def per_device(embeddings, assignment, order_key):
    rows, width = embeddings.shape
    n_split = lax.axis_size("split")
    n = lax.axis_size("dp") * n_split
    most = 3 * rows // (2 * n)
    f32, bf16 = jnp.float32, jnp.bfloat16
    vmem = pl.BlockSpec(memory_space=pltpu.VMEM)
    dma = pltpu.SemaphoreType.DMA((n,))
    nearest = pl.pallas_call(
        functools.partial(kernel, n, n_split, most),
        out_shape=jax.ShapeDtypeStruct((1, rows), f32),
        in_specs=[vmem] * 3,
        out_specs=vmem,
        scratch_shapes=[
            pltpu.VMEM((1, rows), jnp.int32),
            pltpu.VMEM((n, most, width), bf16),
            pltpu.VMEM((n, SUB, most), f32),
            pltpu.VMEM((n, most, width), bf16),
            pltpu.VMEM((n, SUB, most), f32),
            pltpu.VMEM((n, SUB, most), f32),
            pltpu.VMEM((n, most, 128), f32),
            pltpu.VMEM((n, SUB, most), f32),
            pltpu.VMEM((n, SUB, most), f32),
            pltpu.VMEM((n, SUB, most), f32),
            dma, dma, dma, dma, dma, dma,
        ],
        compiler_params=pltpu.CompilerParams(collective_id=0, has_side_effects=True, vmem_limit_bytes=56 * 1024 * 1024),
    )(embeddings, assignment.reshape(1, rows), order_key.reshape(1, rows))
    return nearest.reshape(rows)


def solution(mesh):
    placed = (
        P(("groups", "dp", "split"), None),
        P(("groups", "dp", "split"), None),
        P(("groups", "dp", "split")),
    )
    return jax.shard_map(
        per_device,
        mesh=mesh,
        in_specs=placed,
        out_specs=P(("groups", "dp", "split")),
        check_vma=False,
    )
```

time: 205 us -> 101 us (0.49)
  Pallas kernels: 0 us -> 99.4 us
  blocking collectives: 79.6 us -> 0 us
  local copies, waits for them, and re-layouts: 35.7 us -> 1.3 us
  other arithmetic: 20.9 us -> 0 us
  matrix products: 19.5 us -> 0 us
  loops' own time: 15.3 us -> 0 us
  between operations: 13.5 us -> 0.01 us
  waiting for transfers between devices: 13.1 us -> 0 us
  starting transfers between devices: 6.93 us -> 0 us
    pallas_call x0 -> x1, Pallas kernels: none -> 99.4 us  [per_device(): pl.pallas_call(functools.partial(kernel, n, n_split, most), out_shape=jax...]
    all_to_all x1 -> x0, blocking collectives: 77.8 us -> none  [per_device(): lax.all_to_all(send_rows, 'dp', split_axis=0, concat_axis=0, tiled=True)]
    gather x1 -> x0, local copies, waits for them, and re-layouts: 20.5 us -> none  [per_device(): return returned.reshape(clusters * most)[slot]]
    dot_general x4 -> x0, matrix products: 19.5 us -> none  [step(): lax.dot_general(own_blocks[index], cols[which], (((1,), (1,)), ((), ())),...]
    another operation x1 -> x0, loops' own time: 15.3 us -> none  [tile_max(): return lax.map(step, jnp.arange(count * 2)).reshape(count, length)]
    all_to_all x2 -> x0, waiting for transfers between devices: 13.1 us -> none  [the longest x1 6.57 us: per_device(): lax.all_to_all(send_keys, 'dp', split_axis=0, concat_axis=0, tiled=True)]
    scatter x1 -> x0, other arithmetic: 11.8 us -> none  [per_device(): jnp.zeros((clusters * most, width), jnp.bfloat16).at[slot].set(unit)]
    scatter x1 -> x0, local copies, waits for them, and re-layouts: 8.22 us -> none  [per_device(): jnp.full((clusters * most,), empty_key, jnp.int32).at[slot].set(order_key)]
  transfers between devices with their start and end apart: 3 -> 0, of which waited for: 2 -> 0; matrix products, arithmetic and copies ran while one was open for 4% -> 0% of each run, Pallas kernels for 0% -> 0%
where the time goes in v1:
time: 101 us
  Pallas kernels  99.4 us (98%)
  local copies, waits for them, and re-layouts  1.3 us (1%)
    pallas_call x1, Pallas kernels, per_device(): pl.pallas_call(functools.partial(kernel, n, n_split, most), out_shape=jax...  99.4 us

profile of v1, /device:TPU:0, one launch (start us, length us, event | category | flops | bytes accessed | tf_op | source)
XLA Modules:
  0.0 100.7 jit_solution(1310817856902255089)
XLA Ops:
  0.0 99.4 %shard_map.37 = f32[1,2048]{1,0:T(1,128)} custom-call(bf16[2048,512]{1,0:T(8,128)(2,1)} %rows_ref.1, s32[1,2048]{1,0:T(1,128)} %bitcast.4, s32[1,2048]{1,0:T(1,128)} %bitcast.5), custom_call_target="tpu_custom_call" | custom-call | tf_op jit(solution)/shard_map/pallas_call | solution.py:181
  99.4 1.3 %copy.5 = f32[2048]{0:T(1024)} copy(f32[2048]{0:T(1024)} %bitcast.3) | data formatting | bytes 16384

commit v2 on v1

--- a/solution.py
+++ b/solution.py
@@ -12,6 +12,7 @@
 NT = (((1,), (1,)), ((), ()))
 BLOCK = 256
 SUB = 8
+GROUP = 4
 
 
 def xor(a, b, n):
@@ -102,7 +103,7 @@
         parts = digits_in.astype(bf16)
         lane_key[slot] = jnp.dot(weights((SUB, SUB), 1), parts, preferred_element_type=f32)
         turned = lax.dot_general(identity, parts, NT, preferred_element_type=f32).astype(bf16)
-        sub_key[slot] = jnp.dot(turned, weights((SUB, 128), 0), preferred_element_type=f32)
+        sub_key[slot] = jnp.dot(turned, weights((SUB, most), 0), preferred_element_type=f32)
 
     def tile(columns, columns_key, own, own_key):
         sims = lax.dot_general(columns, own, NT, preferred_element_type=f32)
@@ -111,7 +112,7 @@
 
     recv[0] = send[0]
     take(0, send[0], send_key[0])
-    best[0] = jnp.maximum(tile(recv[0], sub_key[0][:, :1], recv[0], lane_key[0][:1]), -1.0)
+    best[0] = jnp.maximum(tile(recv[0], sub_key[0], recv[0], lane_key[0][:1]), -1.0)
 
     @pl.loop(1, n)
     def _(u):
@@ -119,14 +120,20 @@
         key_copy(u).wait_recv()
         new = recv[u]
         take(u, new, recv_key[u])
-        new_lane, new_sub = lane_key[u][:1], sub_key[u][:, :1]
+        new_lane, new_sub = lane_key[u][:1], sub_key[u]
 
         def meet(i, running):
             other = recv[i]
             best[i] = jnp.maximum(best[i], tile(new, new_sub, other, lane_key[i][:1]))
-            return jnp.maximum(running, tile(other, sub_key[i][:, :1], new, new_lane))
-
-        best[u] = lax.fori_loop(0, u, meet, tile(new, new_sub, new, new_lane))
+            return jnp.maximum(running, tile(other, sub_key[i], new, new_lane))
+
+        def meet_group(group, running):
+            for i in range(GROUP):
+                running = meet(group * GROUP + i, running)
+            return running
+
+        running = lax.fori_loop(0, u // GROUP, meet_group, tile(new, new_sub, new, new_lane))
+        best[u] = lax.fori_loop(u // GROUP * GROUP, u, meet, running)
 
     part = lax.broadcasted_iota(i32, (SUB, most), 0)
 
@@ -190,7 +197,7 @@
             pltpu.VMEM((n, most, width), bf16),
             pltpu.VMEM((n, SUB, most), f32),
             pltpu.VMEM((n, SUB, most), f32),
-            pltpu.VMEM((n, most, 128), f32),
+            pltpu.VMEM((n, most, most), f32),
             pltpu.VMEM((n, SUB, most), f32),
             pltpu.VMEM((n, SUB, most), f32),
             pltpu.VMEM((n, SUB, most), f32),

time: 101 us -> 92.1 us (0.912)
  Pallas kernels: 99.4 us -> 90.5 us
    pallas_call x1, Pallas kernels: 99.4 us -> 90.5 us  [per_device(): pl.pallas_call(functools.partial(kernel, n, n_split, most), out_shape=jax...]
where the time goes in v2:
time: 92.1 us; the launch traced here: 91.9 us
  Pallas kernels  90.5 us (98%)
  local copies, waits for them, and re-layouts  1.3 us (1%)
    pallas_call x1, Pallas kernels, per_device(): pl.pallas_call(functools.partial(kernel, n, n_split, most), out_shape=jax...  90.5 us

profile of v2, /device:TPU:0, one launch (start us, length us, event | category | flops | bytes accessed | tf_op | source)
XLA Modules:
  0.0 91.9 jit_solution(14092247804777491374)
XLA Ops:
  0.0 90.5 %shard_map.37 = f32[1,2048]{1,0:T(1,128)} custom-call(bf16[2048,512]{1,0:T(8,128)(2,1)} %rows_ref.1, s32[1,2048]{1,0:T(1,128)} %bitcast.4, s32[1,2048]{1,0:T(1,128)} %bitcast.5), custom_call_target="tpu_custom_call" | custom-call | tf_op jit(solution)/shard_map/pallas_call | solution.py:188
  90.6 1.3 %copy.5 = f32[2048]{0:T(1024)} copy(f32[2048]{0:T(1024)} %bitcast.3) | data formatting | bytes 16384

commit v3 on v2

--- a/solution.py
+++ b/solution.py
@@ -30,11 +30,13 @@
     return (1 - near) * (n // 2 + t // 2) + near * ((t + 1) // 2 % (n // 2))
 
 
-def kernel(n, n_split, most, rows_ref, cluster_ref, key_ref, out_ref,
-           slot_ref, send, send_key, recv, recv_key, lane_key, sub_key, best, back_send, back,
+def kernel(n, n_split, most, rows_hbm, cluster_ref, key_ref, out_ref,
+           rows_ref, rows_sem, slot_ref, send, send_key, recv, recv_key, lane_key, sub_key, best, back_send, back, back_parts,
            row_ssem, row_rsem, key_ssem, key_rsem, back_ssem, back_rsem):
     f32, bf16, i32 = jnp.float32, jnp.bfloat16, jnp.int32
     rows = rows_ref.shape[0]
+    fetch = pltpu.make_async_copy(rows_hbm, rows_ref, rows_sem)
+    fetch.start()
     me = lax.axis_index("dp") * n_split + lax.axis_index("split")
 
     def device(slot):
@@ -63,10 +65,16 @@
     digits = jnp.where(digit == 0, key // 16384, jnp.where(digit == 1, (key // 128) % 128, jnp.where(digit == 2, key % 128, jnp.where(digit == 3, 1, 0))))
     digits = digits.astype(f32).astype(bf16)
 
-    def weights(shape, dim):
-        place = lax.broadcasted_iota(i32, shape, dim)
-        w = jnp.where(place == 0, 16384.0, jnp.where(place == 1, 128.0, jnp.where(place == 2, 1.0, jnp.where(place == 3, -4194304.0, 0.0))))
-        return w.astype(bf16)
+    place = lax.broadcasted_iota(i32, (SUB, SUB), 1)
+    combine = jnp.where(place == 0, 16384.0, jnp.where(place == 1, 128.0, jnp.where(place == 2, 1.0, jnp.where(place == 3, -4194304.0, 0.0)))).astype(bf16)
+    part = lax.broadcasted_iota(i32, (SUB, most), 0)
+
+    def parts_of(row):
+        whole = jnp.broadcast_to(row, (SUB, most))
+        high = whole.astype(bf16).astype(f32)
+        middle = (whole - high).astype(bf16).astype(f32)
+        low = (whole - high) - middle
+        return jnp.where(part == 0, high, jnp.where(part == 1, middle, jnp.where(part == 2, low, 0.0)))
 
     same = lax.broadcasted_iota(i32, (most, most), 0) == lax.broadcasted_iota(i32, (most, most), 1)
     identity = jnp.where(same, 1.0, 0.0).astype(bf16)
@@ -76,7 +84,8 @@
         pick = jnp.where(lax.broadcasted_iota(i32, (most, rows), 0) == place, 1.0, 0.0).astype(bf16)
         values = jnp.dot(pick, rows_ref[...], preferred_element_type=f32)
         scale = lax.rsqrt(jnp.sum(values * values, axis=1, keepdims=True) + epsilon)
-        return (values * scale).astype(bf16), lax.dot_general(digits, pick, NT, preferred_element_type=f32)
+        picked = lax.dot_general(digits, pick, NT, preferred_element_type=f32)
+        return (values * scale).astype(bf16), jnp.dot(combine, picked.astype(bf16), preferred_element_type=f32)[:1]
 
     def row_copy(slot):
         return pltpu.make_async_remote_copy(send.at[slot], recv.at[slot], row_ssem.at[slot], row_rsem.at[slot], device_id=device(slot), device_id_type=MESH)
@@ -87,6 +96,7 @@
     def back_copy(slot, cluster):
         return pltpu.make_async_remote_copy(back_send.at[slot], back.at[cluster], back_ssem.at[slot], back_rsem.at[slot], device_id=device(slot), device_id_type=MESH)
 
+    fetch.wait()
     send[1], send_key[1] = pack(xor(me, offset_of(1, n), n))
     pl.semaphore_wait(barrier, n - 1)
 
@@ -99,11 +109,10 @@
         send[at] = packed
         send_key[at] = packed_key
 
-    def take(slot, new, digits_in):
-        parts = digits_in.astype(bf16)
-        lane_key[slot] = jnp.dot(weights((SUB, SUB), 1), parts, preferred_element_type=f32)
-        turned = lax.dot_general(identity, parts, NT, preferred_element_type=f32).astype(bf16)
-        sub_key[slot] = jnp.dot(turned, weights((SUB, most), 0), preferred_element_type=f32)
+    def take(slot, row):
+        lane_key[slot] = jnp.broadcast_to(row, (SUB, most))
+        turned = lax.dot_general(identity, parts_of(row).astype(bf16), NT, preferred_element_type=f32).astype(bf16)
+        sub_key[slot] = jnp.dot(turned, jnp.ones((SUB, most), bf16), preferred_element_type=f32)
 
     def tile(columns, columns_key, own, own_key):
         sims = lax.dot_general(columns, own, NT, preferred_element_type=f32)
@@ -111,7 +120,7 @@
         return jnp.max(seen.reshape(most // SUB, SUB, most), axis=0)
 
     recv[0] = send[0]
-    take(0, send[0], send_key[0])
+    take(0, send_key[0])
     best[0] = jnp.maximum(tile(recv[0], sub_key[0], recv[0], lane_key[0][:1]), -1.0)
 
     @pl.loop(1, n)
@@ -119,7 +128,7 @@
         row_copy(u).wait_recv()
         key_copy(u).wait_recv()
         new = recv[u]
-        take(u, new, recv_key[u])
+        take(u, recv_key[u])
         new_lane, new_sub = lane_key[u][:1], sub_key[u]
 
         def meet(i, running):
@@ -135,20 +144,11 @@
         running = lax.fori_loop(0, u // GROUP, meet_group, tile(new, new_sub, new, new_lane))
         best[u] = lax.fori_loop(u // GROUP * GROUP, u, meet, running)
 
-    part = lax.broadcasted_iota(i32, (SUB, most), 0)
-
-    def parts_of(slot):
-        whole = jnp.broadcast_to(jnp.max(best[slot], axis=0, keepdims=True), (SUB, most))
-        high = whole.astype(bf16).astype(f32)
-        middle = (whole - high).astype(bf16).astype(f32)
-        low = (whole - high) - middle
-        return jnp.where(part == 0, high, jnp.where(part == 1, middle, jnp.where(part == 2, low, 0.0)))
-
-    @pl.loop(1, n)
-    def _(slot):
-        back_send[slot] = parts_of(slot)
-
-    back[me] = parts_of(0)
+    @pl.loop(1, n)
+    def _(slot):
+        back_send[slot] = jnp.max(best[slot], axis=0, keepdims=True)
+
+    back_parts[me] = parts_of(jnp.max(best[0], axis=0, keepdims=True))
 
     @pl.loop(1, n)
     def _(slot):
@@ -161,9 +161,11 @@
 
     @pl.loop(1, n)
     def _(slot):
-        back_copy(slot, xor(me, offset_of(slot, n), n)).wait_recv()
-
-    turned = lax.dot_general(identity, back[...].reshape(n * SUB, most).astype(bf16), NT, preferred_element_type=f32).astype(bf16)
+        cluster = xor(me, offset_of(slot, n), n)
+        back_copy(slot, cluster).wait_recv()
+        back_parts[cluster] = parts_of(back[cluster])
+
+    turned = lax.dot_general(identity, back_parts[...].reshape(n * SUB, most).astype(bf16), NT, preferred_element_type=f32).astype(bf16)
     for start in range(0, rows, BLOCK):
         here = cluster_ref[:, start:start + BLOCK]
         rank = slot_ref[:, start:start + BLOCK] - here * most
@@ -188,18 +190,21 @@
     nearest = pl.pallas_call(
         functools.partial(kernel, n, n_split, most),
         out_shape=jax.ShapeDtypeStruct((1, rows), f32),
-        in_specs=[vmem] * 3,
+        in_specs=[pl.BlockSpec(memory_space=pl.ANY), vmem, vmem],
         out_specs=vmem,
         scratch_shapes=[
+            pltpu.VMEM((rows, width), bf16),
+            pltpu.SemaphoreType.DMA,
             pltpu.VMEM((1, rows), jnp.int32),
             pltpu.VMEM((n, most, width), bf16),
-            pltpu.VMEM((n, SUB, most), f32),
+            pltpu.VMEM((n, 1, most), f32),
             pltpu.VMEM((n, most, width), bf16),
-            pltpu.VMEM((n, SUB, most), f32),
+            pltpu.VMEM((n, 1, most), f32),
             pltpu.VMEM((n, SUB, most), f32),
             pltpu.VMEM((n, most, most), f32),
             pltpu.VMEM((n, SUB, most), f32),
-            pltpu.VMEM((n, SUB, most), f32),
+            pltpu.VMEM((n, 1, most), f32),
+            pltpu.VMEM((n, 1, most), f32),
             pltpu.VMEM((n, SUB, most), f32),
             dma, dma, dma, dma, dma, dma,
         ],

time: 92.1 us -> 89.4 us (0.971)
  Pallas kernels: 90.5 us -> 87.7 us
    pallas_call x1, Pallas kernels: 90.5 us -> 87.7 us  [per_device(): pl.pallas_call(functools.partial(kernel, n, n_split, most), out_shape=jax...]
where the time goes in v3:
time: 89.4 us; the launch traced here: 89 us
  Pallas kernels  87.7 us (98%)
  local copies, waits for them, and re-layouts  1.3 us (1%)
    pallas_call x1, Pallas kernels, per_device(): pl.pallas_call(functools.partial(kernel, n, n_split, most), out_shape=jax...  87.7 us

profile of v3, /device:TPU:0, one launch (start us, length us, event | category | flops | bytes accessed | tf_op | source)
XLA Modules:
  0.0 89.0 jit_solution(14189225225348550471)
XLA Ops:
  0.0 87.7 %shard_map.37 = f32[1,2048]{1,0:T(1,128)} custom-call(bf16[2048,512]{1,0:T(8,128)(2,1)} %rows_hbm.1, s32[1,2048]{1,0:T(1,128)} %bitcast.4, s32[1,2048]{1,0:T(1,128)} %bitcast.5), custom_call_target="tpu_custom_call" | custom-call | tf_op jit(solution)/shard_map/pallas_call | solution.py:190
  87.7 1.3 %copy.5 = f32[2048]{0:T(1024)} copy(f32[2048]{0:T(1024)} %bitcast.3) | data formatting | bytes 16384

commit v4 on v3

--- a/solution.py
+++ b/solution.py
@@ -12,7 +12,7 @@
 NT = (((1,), (1,)), ((), ()))
 BLOCK = 256
 SUB = 8
-GROUP = 4
+GROUP = 5
 
 
 def xor(a, b, n):
@@ -26,8 +26,10 @@
 
 def offset_of(slot, n):
     t = slot - 1
-    near = t % 2
-    return (1 - near) * (n // 2 + t // 2) + near * ((t + 1) // 2 % (n // 2))
+    h = n // 2
+    far = slot // (h + 2)
+    first = (h + 2 - slot) // h
+    return (1 - far) * (first * (h + t) + (1 - first) * (t - 1)) + far * (slot % n)
 
 
 def kernel(n, n_split, most, rows_hbm, cluster_ref, key_ref, out_ref,
@@ -144,15 +146,15 @@
         running = lax.fori_loop(0, u // GROUP, meet_group, tile(new, new_sub, new, new_lane))
         best[u] = lax.fori_loop(u // GROUP * GROUP, u, meet, running)
 
-    @pl.loop(1, n)
-    def _(slot):
-        back_send[slot] = jnp.max(best[slot], axis=0, keepdims=True)
-
+    back_send[n - 1] = jnp.max(best[n - 1], axis=0, keepdims=True)
+
+    @pl.loop(2, n)
+    def _(step):
+        back_send[n - step] = jnp.max(best[n - step], axis=0, keepdims=True)
+        back_copy(n - step + 1, me).start()
+
+    back_copy(1, me).start()
     back_parts[me] = parts_of(jnp.max(best[0], axis=0, keepdims=True))
-
-    @pl.loop(1, n)
-    def _(slot):
-        back_copy(slot, me).start()
 
     @pl.loop(1, n)
     def _(slot):

time: 89.4 us -> 87.1 us (0.974)
  Pallas kernels: 87.7 us -> 85.5 us
    pallas_call x1, Pallas kernels: 87.7 us -> 85.5 us  [per_device(): pl.pallas_call(functools.partial(kernel, n, n_split, most), out_shape=jax...]
where the time goes in v4:
time: 87.1 us; the launch traced here: 86.8 us
  Pallas kernels  85.5 us (98%)
  local copies, waits for them, and re-layouts  1.3 us (1%)
    pallas_call x1, Pallas kernels, per_device(): pl.pallas_call(functools.partial(kernel, n, n_split, most), out_shape=jax...  85.5 us

profile of v4, /device:TPU:0, one launch (start us, length us, event | category | flops | bytes accessed | tf_op | source)
XLA Modules:
  0.0 86.8 jit_solution(1951884632496194151)
XLA Ops:
  0.0 85.5 %shard_map.37 = f32[1,2048]{1,0:T(1,128)} custom-call(bf16[2048,512]{1,0:T(8,128)(2,1)} %rows_hbm.1, s32[1,2048]{1,0:T(1,128)} %bitcast.4, s32[1,2048]{1,0:T(1,128)} %bitcast.5), custom_call_target="tpu_custom_call" | custom-call | tf_op jit(solution)/shard_map/pallas_call | solution.py:192
  85.5 1.3 %copy.5 = f32[2048]{0:T(1024)} copy(f32[2048]{0:T(1024)} %bitcast.3) | data formatting | bytes 16384

commit v5 on v4

--- a/solution.py
+++ b/solution.py
@@ -27,9 +27,9 @@
 def offset_of(slot, n):
     t = slot - 1
     h = n // 2
-    far = slot // (h + 2)
-    first = (h + 2 - slot) // h
-    return (1 - far) * (first * (h + t) + (1 - first) * (t - 1)) + far * (slot % n)
+    far = slot // (h + 3)
+    first = (h + 3 - slot) // h
+    return (1 - far) * (first * (h + t) + (1 - first) * (t - 2)) + far * (slot % n)
 
 
 def kernel(n, n_split, most, rows_hbm, cluster_ref, key_ref, out_ref,

time: 87.1 us -> 87.3 us (level)
  no operation moved by 1% of the time
where the time goes in v5:
time: 87.3 us; the launch traced here: 87 us
  Pallas kernels  85.7 us (98%)
  local copies, waits for them, and re-layouts  1.3 us (1%)
    pallas_call x1, Pallas kernels, per_device(): pl.pallas_call(functools.partial(kernel, n, n_split, most), out_shape=jax...  85.7 us

profile of v5, /device:TPU:0, one launch (start us, length us, event | category | flops | bytes accessed | tf_op | source)
XLA Modules:
  0.0 87.0 jit_solution(14055602549639296010)
XLA Ops:
  0.0 85.7 %shard_map.37 = f32[1,2048]{1,0:T(1,128)} custom-call(bf16[2048,512]{1,0:T(8,128)(2,1)} %rows_hbm.1, s32[1,2048]{1,0:T(1,128)} %bitcast.4, s32[1,2048]{1,0:T(1,128)} %bitcast.5), custom_call_target="tpu_custom_call" | custom-call | tf_op jit(solution)/shard_map/pallas_call | solution.py:192
  85.7 1.3 %copy.5 = f32[2048]{0:T(1024)} copy(f32[2048]{0:T(1024)} %bitcast.3) | data formatting | bytes 16384
